TPU v7x, 256 devices: a whole 4x4x8 slice. The times are simulated.
256 devices in a mesh: region: 2 (over core), cells: 128 (over z, y, x).
Axes of the slice: x: 4, y: 4, z: 8, core: 2. Of those that a mesh axis runs over, the one named last changes fastest.
Arguments:
- moments: float32 [2, 6, 4, 128, 16384], P('region', None, None, None, 'cells'), may hold values from 0 to 40, as said below
- courant_azimuth: float32 [2, 4, 128, 16384], P('region', None, None, 'cells'), may hold values from 0.1 to 0.3
- courant_radial: float32 [2, 4, 128, 16384], P('region', None, None, 'cells'), may hold values from -0.25 to 0.25
- courant_axial: float32 [2, 4, 128, 16384], P('region', None, None, 'cells'), may hold values from -0.2 to 0.2
- shear: float32 [2, 4, 128, 16384], P('region', None, None, 'cells'), may hold values from 0.5 to 4
- owner: int32 [2, 16384, 1], P('region', 'cells'), may hold values from 0 to 127; in each aligned block of 128 rows (0 to 127, 128 to 255, ..., all dimensions but the last counted through in order) at most 2 rows name the same one
- target: int32 [2, 16384], P('region', 'cells'), may hold values from 0 to 127
- ami_weight: float32 [2, 16384, 128, 128], P('region', 'cells'), may hold values from 0 to 1, as said below
Outputs:
- updated: float32 [2, 6, 4, 128, 16384], P('region', None, None, None, 'cells')
Inputs may be any that keep to these rules, and one draw needn't show every extreme that they name: The rows of one device name each owner at most 2 times. Each cell's six entries are the moments of orders 0 to 5 of a positive measure on three or more sizes between 0.3 and 1.6. `ami_weight`: all entries are nonnegative.
All inputs are finite; a program needn't handle non-finite values.
Results may differ from a plain program's by a relative error of at most 0.0003.
Values sent between devices are 32-bit elements; how exact they have to be, the bound alone decides.
A program may use at most 64 MiB of HBM per device.

v0:
```python
import math

import jax
import jax.numpy as jnp
from jax import lax
from jax.sharding import PartitionSpec as P

KAGG = 0.005
KBRK = 0.02


def from_partner(shard, axis, bit):
    return lax.ppermute(shard, axis, [(i, i ^ 1 << bit) for i in range(lax.axis_size(axis))])


def shifted(shard, axis, by):
    count = lax.axis_size(axis)
    return lax.ppermute(shard, axis, [(i, (i + by) % count) for i in range(count)])


def quadrature(moment):
    mass = moment[0]
    scaled = [moment[degree] / mass for degree in range(6)]
    mean_size = scaled[1]
    first_two = scaled[2] - mean_size * scaled[1]
    first_three = scaled[3] - mean_size * scaled[2]
    first_four = scaled[4] - mean_size * scaled[3]
    first_five = scaled[5] - mean_size * scaled[4]
    alpha_one = first_three / first_two - mean_size
    second_two = first_four - alpha_one * first_three - first_two * scaled[2]
    second_three = first_five - alpha_one * first_four - first_two * scaled[3]
    alpha_two = second_three / second_two - first_three / first_two
    beta_two = second_two / first_two
    centre = (mean_size + alpha_one + alpha_two) / 3.0
    dev_zero = mean_size - centre
    dev_one = alpha_one - centre
    dev_two = alpha_two - centre
    spread = jnp.sqrt(
        (dev_zero * dev_zero + dev_one * dev_one + dev_two * dev_two + 2.0 * (first_two + beta_two))
        / 6.0
    )
    determ = dev_zero * (dev_one * dev_two - beta_two) - first_two * dev_two
    cosine = jnp.clip(determ / (2.0 * spread * spread * spread), -1.0, 1.0)
    third = jnp.arccos(cosine) / 3.0
    node_high = centre + 2.0 * spread * jnp.cos(third)
    node_low = centre + 2.0 * spread * jnp.cos(third + 2.0 * math.pi / 3.0)
    node_mid = 3.0 * centre - node_high - node_low
    nodes = [node_low, node_mid, node_high]
    weights = []
    for node in nodes:
        lead = node - mean_size
        trail = (node - alpha_one) * lead - first_two
        norm_sq = 1.0 + lead * lead / first_two + trail * trail / (first_two * beta_two)
        weights.append(mass / norm_sq)
    return (nodes, weights)


def sources(moment, shear):
    nodes, weights = quadrature(moment)
    cubes = [node * node * node for node in nodes]
    pairs = []
    for first in range(3):
        for second in range(3):
            summed = nodes[first] + nodes[second]
            kernel = shear * summed * summed * summed
            pairs.append(
                (
                    first,
                    second,
                    weights[first] * weights[second] * kernel,
                    jnp.log(cubes[first] + cubes[second]),
                )
            )
    result = []
    for degree in range(6):
        birth = jnp.zeros_like(shear)
        death = jnp.zeros_like(shear)
        for first, second, pair, logsum in pairs:
            birth = birth + 0.5 * pair * jnp.exp(degree / 3.0 * logsum)
            death = death + pair * nodes[first] ** degree
        factor = 2.0 ** (1.0 - degree / 3.0) - 1.0
        breakage = jnp.zeros_like(shear)
        for index in range(3):
            breakage = (
                breakage
                + weights[index] * KBRK * shear * cubes[index] * factor * nodes[index] ** degree
            )
        result.append(moment[degree] + KAGG * (birth - death) + breakage)
    return jnp.stack(result)


def advance(moment, previous, ghost_layer, is_rotor, azim, radial, axial, shear):
    empty_layer = jnp.zeros_like(ghost_layer)
    beyond_edge = jnp.where(is_rotor, ghost_layer, empty_layer)
    below_edge = jnp.where(is_rotor, empty_layer, ghost_layer)
    prev_azim = jnp.concatenate([previous[..., None], moment[..., :-1]], axis=3)
    radial_below = jnp.concatenate([below_edge[:, None], moment[:, :-1]], axis=1)
    radial_beyond = jnp.concatenate([moment[:, 1:], beyond_edge[:, None]], axis=1)
    axial_pad = jnp.zeros_like(moment[:, :, :1])
    axial_below = jnp.concatenate([axial_pad, moment[:, :, :-1]], axis=2)
    axial_beyond = jnp.concatenate([moment[:, :, 1:], axial_pad], axis=2)
    advected = (
        moment
        - azim * (moment - prev_azim)
        - jnp.maximum(radial, 0.0) * (moment - radial_below)
        - jnp.minimum(radial, 0.0) * (radial_beyond - moment)
        - jnp.maximum(axial, 0.0) * (moment - axial_below)
        - jnp.minimum(axial, 0.0) * (axial_beyond - moment)
    )
    return sources([advected[degree] for degree in range(6)], shear)


def collect(received, received_rows, row_count):
    hits = (jnp.arange(row_count)[:, None] == received_rows[None, :]).astype(jnp.float32)
    summed = jnp.dot(
        hits, received, precision=lax.Precision.HIGHEST, preferred_element_type=jnp.float32
    )
    return summed.reshape(row_count, 6, -1).transpose(1, 0, 2)


def on_device(
    moments, courant_azimuth, courant_radial, courant_axial, shear, owner, target, ami_weight
):
    moment = moments[0]
    layer_count = moment.shape[1]
    row_count = moment.shape[2]
    face_count = moment.shape[3]
    peers = lax.axis_size("cells")
    capacity = max(2, 2 * row_count // peers)
    is_rotor = lax.axis_index("region") == 0
    layer = jnp.where(is_rotor, moment[:, layer_count - 1], moment[:, 0])
    contrib = jnp.einsum("zfg,kzg->zkf", ami_weight[0], layer, precision=lax.Precision.HIGHEST)
    owners = owner[0, :, 0]
    rows_to = target[0]
    order_idx = jnp.arange(row_count)
    same_owner = owners[:, None] == owners[None, :]
    earlier = order_idx[None, :] < order_idx[:, None]
    rank = jnp.sum(jnp.logical_and(same_owner, earlier).astype(jnp.int32), axis=1)
    destination = owners * capacity + rank
    slot_ids = jnp.arange(peers * capacity)
    picked = slot_ids[:, None] == destination[None, :]
    outgoing = jnp.dot(
        picked.astype(jnp.float32),
        contrib.reshape(row_count, 6 * face_count),
        precision=lax.Precision.HIGHEST,
        preferred_element_type=jnp.float32,
    )
    outgoing_rows = jnp.sum(jnp.where(picked, rows_to[None, :], 0), axis=1)
    received, received_rows = (
        lax.all_to_all(outgoing, "cells", split_axis=0, concat_axis=0, tiled=True),
        lax.all_to_all(outgoing_rows, "cells", split_axis=0, concat_axis=0, tiled=True),
    )
    other_ghost = collect(received, received_rows, row_count)
    ghost_layer = from_partner(other_ghost, "region", 0)
    rim = moment[:, :, :, face_count - 1]
    previous = shifted(rim, "cells", 1)
    updated = advance(
        moment,
        previous,
        ghost_layer,
        is_rotor,
        courant_azimuth[0],
        courant_radial[0],
        courant_axial[0],
        shear[0],
    )
    return updated[None]


def solution(mesh):
    placed = (
        P("region", None, None, None, "cells"),
        P("region", None, None, "cells"),
        P("region", None, None, "cells"),
        P("region", None, None, "cells"),
        P("region", None, None, "cells"),
        P("region", "cells", None),
        P("region", "cells"),
        P("region", "cells", None, None),
    )
    return jax.shard_map(
        on_device,
        mesh=mesh,
        in_specs=placed,
        out_specs=P("region", None, None, None, "cells"),
        check_vma=False,
    )
```

profile of v0, /device:TPU:1, one launch (start us, length us, event | category | flops | bytes accessed | tf_op | source)
XLA Modules:
  0.0 99.3 jit_solution(14807917610526953947)
XLA Ops:
  0.0 0.9 convert_reduce_fusion
  0.9 0.7 multiply_add_fusion.4
  1.6 0.8 select_reduce_fusion
  2.3 0.8 all_to_all.12
  3.1 16.3 %all-to-all-start = ((s32[128,2,1]{1,2,0:T(1,128)}), s32[128,2,1]{1,2,0:T(1,128)S(1)}, u32[]{:S(2)}, u32[]{:S(2)}) async-start(s32[128,2,1]{1,2,0:T(1,128)} %bitcast.6), calls=%async_computation | async-start | bytes 131072 | tf_op jit(solution)/shard_map/all_to_all | solution.py:151
  19.5 1.2 %fusion.11 = f32[6,128,128]{2,1,0:T(8,128)S(1)} fusion(f32[6,4,128,128]{3,2,1,0:T(8,128)} %bitcast.44, pred[]{:T(512)S(6)} %eq.61), kind=kLoop, calls=%fused_computation.17 | loop fusion | flops 98304 | bytes 1179649 | tf_op jit(solution)/shard_map/jit(_where)/select_n | solution.py:131
  20.7 15.4 %fusion = f32[128,6,128]{2,1,0:T(8,128)S(1)} fusion(f32[1,128,128,128]{3,2,1,0:T(8,128)} %param.15, f32[6,128,128]{2,1,0:T(8,128)S(1)} %fusion.11), kind=kOutput, calls=%fused_computation | convolution fusion | flops 150994944 | bytes 9175040 | tf_op jit(solution)/shard_map/zfg,kzg->zkf/dot_general | solution.py:132
  36.1 0.2 copy.41
  36.3 0.5 fusion.105
  36.8 0.0 copy-start
  36.8 1.5 %copy.43 = f32[128,2,768]{2,1,0:T(2,128)} copy(f32[128,2,768]{2,0,1:T(8,128)S(1)} %fusion.105) | data formatting | bytes 1572864 | tf_op jit(solution)/shard_map/dot_general | solution.py:142
  38.3 0.0 all-to-all-done
  38.3 13.2 %all-to-all-start.1 = ((f32[128,2,768]{2,1,0:T(2,128)}), f32[128,2,768]{2,1,0:T(2,128)S(1)}, u32[]{:S(2)}, u32[]{:S(2)}) async-start(f32[128,2,768]{2,1,0:T(2,128)} %copy.43), calls=%async_computation.1 | async-start | bytes 1572864 | tf_op jit(solution)/shard_map/all_to_all | solution.py:150
  51.5 0.0 copy-done
  51.5 0.9 slice_reduce_fusion
  52.4 0.8 collective-permute-start
  53.3 2.0 %fusion.120 = (f32[6,4,127,128]{3,2,1,0:T(8,128)}, f32[6,4,127,128]{3,2,1,0:T(8,128)}) fusion(f32[6,4,128,128]{3,2,1,0:T(8,128)S(1)} %bitcast.46), kind=kLoop, calls=%fused_computation.181 | loop fusion | bytes 6242304 | tf_op jit(solution)/shard_map/slice | solution.py:100
  55.2 0.6 broadcast.324
  55.8 0.8 reduce.5
  56.7 0.1 eq.69
  56.8 17.6 %all-to-all-done.1 = f32[128,2,768]{2,1,0:T(2,128)S(1)} async-done(((f32[128,2,768]{2,1,0:T(2,128)}), f32[128,2,768]{2,1,0:T(2,128)S(1)}, u32[]{:S(2)}, u32[]{:S(2)}) %all-to-all-start.1) | async-done | bytes 786464 | tf_op jit(solution)/shard_map/all_to_all | solution.py:150
  74.4 0.5 all_to_all.15
  75.0 0.3 copy.44
  75.3 1.3 %convolution_bitcast_fusion = f32[6,128,128]{2,1,0:T(8,128)} fusion(f32[6,128,256]{2,1,0:T(8,128)S(1)} %bitcast.50, s32[256]{0:T(256)S(1)} %eq.69), kind=kOutput, calls=%fused_computation.14 | convolution fusion | flops 302022656 | bytes 1180672 | tf_op jit(solution)/shard_map/dot_general | solution.py:115
  76.6 4.1 %collective-permute-start.1 = (f32[6,128,128]{2,1,0:T(8,128)}, f32[6,128,128]{2,1,0:T(8,128)}, u32[]{:S(2)}, u32[]{:S(2)}) collective-permute-start(f32[6,128,128]{2,1,0:T(8,128)} %convolution_bitcast_fusion), channel_id=1, source_target_pairs={{0,128},{128,0},{1,129},{129,1},{2,130},{130,2},{3,131},{131,3},{4... | collective-permute-start | bytes 1179656 | tf_op jit(solution)/shard_map/ppermute | solution.py:13
  80.7 1.7 %fusion.121 = (f32[6,3,128,128]{3,2,1,0:T(8,128)}, f32[6,3,128,128]{3,2,1,0:T(8,128)}) fusion(f32[6,4,128,128]{3,2,1,0:T(8,128)S(1)} %bitcast.47), kind=kLoop, calls=%fused_computation.182 | loop fusion | bytes 4718592 | tf_op jit(solution)/shard_map/slice | solution.py:98
  82.4 0.0 copy-done.3
  82.4 0.0 copy-done.4
  82.4 1.0 maximum_bitcast_fusion
  83.3 0.0 collective-permute-done
  83.3 0.5 copy.38
  83.9 0.0 copy-start.1
  83.9 0.0 collective-permute-done.1
  83.9 1.2 %select_bitcast_fusion = (f32[6,1,128,128]{3,2,1,0:T(8,128)S(1)}, f32[6,1,128,128]{3,2,1,0:T(8,128)S(1)}) fusion(f32[6,128,128]{2,1,0:T(8,128)} %collective-permute-done.1, pred[]{:T(512)S(6)} %eq.61), kind=kLoop, calls=%fused_computation.25 | loop fusion | flops 196608 | bytes 1179649 | tf_op jit(solution)/shard_map/broadcast_in_dim | solution.py:98
  85.0 0.2 copy-done.1
  85.3 3.8 %fusion.7 = f32[6,4,128,128]{3,2,1,0:T(8,128)S(1)} fusion(f32[6,4,128,127]{3,2,1,0:T(8,128)S(1)} %bitcast.48, f32[6,4,128,1]{3,2,1,0:T(8,128)S(1)} %copy.38, f32[6,3,128,128]{3,2,1,0:T(8,128)} %get-tuple-element.29, f32[6,1,128,128]{3,2,1,0:T(8,128)S(1)} %get-tuple-element.31, f32[6,1,128,128]{3,2,1,0:T(8,128)S(1)} %get-tuple-element.30, ...), kind=kLoop, calls=%fused_computation.9 | loop fusion | flops 7077888 | bytes 12296192 | tf_op jit(solution)/shard_map/sub | solution.py:103
  89.0 0.3 divide_subtract_fusion
  89.3 3.0 %add_divide_fusion.1 = (f32[1,4,128,128]{3,2,1,0:T(8,128)S(1)}, f32[1,4,128,128]{3,2,1,0:T(8,128)S(1)}, f32[1,4,128,128]{3,2,1,0:T(8,128)S(1)}, f32[1,4,128,128]{3,2,1,0:T(8,128)S(1)}, f32[1,4,128,128]{3,2,1,0:T(8,128)S(1)}) fusion(f32[1,4,128,128]{3,2,1,0:T(8,128)S(1)} %get-tuple-element.22, f32[1,4,128,128]{3,2,1,0:T(8,128)S(1)} %get-tuple-element.21, ...), kind=kLoop, calls=%fused_computation.145 | loop fusion | flops 3997696 | bytes 3145728 | tf_op jit(solution)/shard_map/div | solution.py:54
  92.3 0.0 copy-start.2
  92.3 0.3 add_divide_fusion
  92.6 0.6 copy-done.2
  93.2 1.0 %add_dynamic-update-slice_fusion = (f32[6,4,128,128]{3,2,1,0:T(8,128)S(1)}, f32[1,4,128,128]{3,2,1,0:T(8,128)S(1)}, f32[1,4,128,128]{3,2,1,0:T(8,128)S(1)}, f32[...) fusion(f32[1,4,128,128]{3,2,1,0:T(8,128)S(1)} %get-tuple-elemen, ...), kind=kLoop, calls=%fused_computation.127 | loop fusion | flops 6356991 | bytes 4718592
  94.3 0.8 fusion.90
  95.0 0.8 fusion.48
  95.8 0.7 fusion.80
  96.6 0.8 fusion.32
  97.4 0.8 fusion.70
  98.2 1.1 %copy-done.5 = f32[6,4,128,128]{3,2,1,0:T(8,128)} copy-done((f32[6,4,128,128]{3,2,1,0:T(8,128)}, f32[6,4,128,128]{3,2,1,0:T(8,128)S(1)}, u32[]{:S(2)}) %copy-start.5) | copy-done | bytes 1572888
  (4 shorter events, 0.0 us)
Async XLA Ops:
  3.1 35.2 %all-to-all-start = ((s32[128,2,1]{1,2,0:T(1,128)}), s32[128,2,1]{1,2,0:T(1,128)S(1)}, u32[]{:S(2)}, u32[]{:S(2)}) async-start(s32[128,2,1]{1,2,0:T(1,128)} %bitcast.6), calls=%async_computation | async-start | bytes 131072 | tf_op jit(solution)/shard_map/all_to_all | solution.py:151
  36.8 14.7 %copy-start = (f32[1,6,4,128,128]{4,3,2,1,0:T(8,128)S(1)}, f32[1,6,4,128,128]{4,3,2,1,0:T(8,128)}, u32[]{:S(2)}) copy-start(f32[1,6,4,128,128]{4,3,2,1,0:T(8,128)} %param.8) | copy-start | bytes 4718596
  38.3 36.1 %all-to-all-start.1 = ((f32[128,2,768]{2,1,0:T(2,128)}), f32[128,2,768]{2,1,0:T(2,128)S(1)}, u32[]{:S(2)}, u32[]{:S(2)}) async-start(f32[128,2,768]{2,1,0:T(2,128)} %copy.43), calls=%async_computation.1 | async-start | bytes 1572864 | tf_op jit(solution)/shard_map/all_to_all | solution.py:150
  52.4 30.9 %collective-permute-start = (f32[6,4,128]{2,1,0:T(4,128)S(1)}, f32[6,4,128]{2,1,0:T(4,128)S(1)}, u32[]{:S(2)}, u32[]{:S(2)}) collective-permute-start(f32[6,4,128]{2,1,0:T(4,128)S(1)} %slice_reduce_fusion), channel_id=1, source_target_pairs={{0,1},{1,2},{2,3},{3,4},{4,5},{5,6},{6,7},{7,8},{8,9},{9,10},{10,1... | collective-permute-start | bytes 36872 | tf_op jit(solution)/shard_map/ppermute | solution.py:18
  76.6 5.8 %copy-start.3 = (f32[1,4,128,128]{3,2,1,0:T(8,128)S(1)}, f32[1,4,128,128]{3,2,1,0:T(8,128)}, u32[]{:S(2)}) copy-start(f32[1,4,128,128]{3,2,1,0:T(8,128)} %param.11) | copy-start | bytes 786436
  76.6 5.8 %copy-start.4 = (f32[1,4,128,128]{3,2,1,0:T(8,128)S(1)}, f32[1,4,128,128]{3,2,1,0:T(8,128)}, u32[]{:S(2)}) copy-start(f32[1,4,128,128]{3,2,1,0:T(8,128)} %param.10) | copy-start | bytes 786436
  76.6 7.3 %collective-permute-start.1 = (f32[6,128,128]{2,1,0:T(8,128)}, f32[6,128,128]{2,1,0:T(8,128)}, u32[]{:S(2)}, u32[]{:S(2)}) collective-permute-start(f32[6,128,128]{2,1,0:T(8,128)} %convolution_bitcast_fusion), channel_id=1, source_target_pairs={{0,128},{128,0},{1,129},{129,1},{2,130},{130,2},{3,131},{131,3},{4... | collective-permute-start | bytes 1179656 | tf_op jit(solution)/shard_map/ppermute | solution.py:13
  83.9 1.4 %copy-start.1 = (f32[6,3,128,128]{3,2,1,0:T(8,128)S(1)}, f32[6,3,128,128]{3,2,1,0:T(8,128)}, u32[]{:S(2)}) copy-start(f32[6,3,128,128]{3,2,1,0:T(8,128)} %get-tuple-element.28) | copy-start | bytes 3538948
  92.3 1.0 copy-start.2
  98.2 1.1 %copy-start.5 = (f32[6,4,128,128]{3,2,1,0:T(8,128)}, f32[6,4,128,128]{3,2,1,0:T(8,128)S(1)}, u32[]{:S(2)}) copy-start(f32[6,4,128,128]{3,2,1,0:T(8,128)S(1)} %fusion.70) | copy-start | bytes 4718596
where the time goes:
time: 99.6 us; the launch traced here: 99.3 us
  starting transfers between devices  34.5 us (35%)
  other arithmetic  18.7 us (19%)
  waiting for transfers between devices  17.6 us (18%)
  matrix products  17.3 us (17%)
  local copies, waits for them, and re-layouts  11 us (11%)
    all_to_all x1, waiting for transfers between devices, on_device(): lax.all_to_all(outgoing, 'cells', split_axis=0, concat_axis=0, tiled=True)  17.6 us
    all_to_all x1, starting transfers between devices, on_device(): lax.all_to_all(outgoing_rows, 'cells', split_axis=0, concat_axis=0, tiled...  16.3 us
    dot_general x1, matrix products, on_device(): jnp.einsum('zfg,kzg->zkf', ami_weight[0], layer, precision=lax.Precision....  15.4 us
    all_to_all x1, starting transfers between devices, on_device(): lax.all_to_all(outgoing, 'cells', split_axis=0, concat_axis=0, tiled=True)  13.2 us
    ppermute x1, starting transfers between devices, from_partner(): lax.ppermute(shard, axis, [(i, i ^ 1 << bit) for i in range(lax.axis_size...  4.14 us
    unnamed x5, other arithmetic  4.14 us
    sub x1, other arithmetic, advance(): moment - azim * (moment - prev_azim)  3.78 us
    div x2, other arithmetic, quadrature(): weights.append(mass / norm_sq)  3.25 us
  transfers between devices with their start and end apart: 4, of which 1 were waited for; matrix products, arithmetic and copies ran while one was open for 28% of the time, Pallas kernels for 0%

commit v1 on v0

v1 whole, which is shorter than its diff:
```python
import functools

import jax
import jax.numpy as jnp
from jax import lax
from jax.experimental import pallas as pl
from jax.experimental.pallas import tpu as pltpu
from jax.sharding import PartitionSpec as P

MESH = pl.DeviceIdType.MESH
F32 = jnp.float32
BF16 = jnp.bfloat16
KAGG = 0.005
KBRK = 0.02
LAYERS = 4
ROWS = 128
FACES = 128
MOMENTS = 6
PEERS = 128
SLOTS = 2
MESSAGE = SLOTS * MOMENTS + 1
PLANE = ROWS + 16
CHUNKS = 8
BLOCK = 16
CUBE_ROOT_2 = 2.0 ** (1.0 / 3.0)

THIRD_ANGLE = (
    0.5000000032577528,
    0.5773497198231888,
    -0.11109568329657703,
    0.053288656003267744,
    -0.03196129546407778,
    0.019675718215576045,
    -0.01032549308338918,
    0.003707686483927317,
    -0.0006393143691536856,
)


def third_angle(s):
    value = THIRD_ANGLE[-1] * s + THIRD_ANGLE[-2]
    for coefficient in THIRD_ANGLE[-3::-1]:
        value = value * s + coefficient
    return value


def quadrature(moment):
    mass = moment[0]
    inverse = 1.0 / mass
    n1, n2, n3, n4, n5 = [moment[degree] * inverse for degree in range(1, 6)]
    a0 = n1
    p1 = n2 - a0 * n1
    p2 = n3 - a0 * n2
    p3 = n4 - a0 * n3
    p4 = n5 - a0 * n4
    over_p1 = 1.0 / p1
    ratio = p2 * over_p1
    a1 = ratio - a0
    q2 = p3 - a1 * p2 - p1 * n2
    q3 = p4 - a1 * p3 - p1 * n3
    over_q2 = 1.0 / q2
    a2 = q3 * over_q2 - ratio
    b2 = q2 * over_p1
    centre = (a0 + a1 + a2) * (1.0 / 3.0)
    d0 = a0 - centre
    d1 = a1 - centre
    d2 = a2 - centre
    square = (d0 * d0 + d1 * d1 + d2 * d2 + 2.0 * (p1 + b2)) * (1.0 / 6.0)
    over_h = lax.rsqrt(square)
    h2 = 2.0 * square * over_h
    determ = d0 * (d1 * d2 - b2) - p1 * d2
    half_cosine = jnp.clip(0.25 * determ * (over_h * over_h * over_h), -0.5, 0.5)
    high = centre + h2 * third_angle(jnp.sqrt(0.5 + half_cosine))
    low = centre - h2 * third_angle(jnp.sqrt(0.5 - half_cosine))
    middle = 3.0 * centre - high - low
    nodes = [low, middle, high]
    weights = []
    for node in nodes:
        lead = node - a0
        trail = (node - a1) * lead - p1
        weights.append(mass / (1.0 + lead * lead * over_p1 + trail * trail * over_q2))
    return nodes, weights


def sources(moment, shear):
    nodes, weights = quadrature(moment)
    cubes = [node * node * node for node in nodes]
    merge = KAGG * shear
    split = KBRK * shear
    carried = [w * c for w, c in zip(weights, cubes)]
    born = [4.0 * w * a * merge for w, a in zip(weights, carried)]
    broken = [split * a for a in carried]
    lost = [2.0 * b + f for b, f in zip(born, broken)]
    terms, steps = [], []
    for first, second in ((0, 1), (0, 2), (1, 2)):
        summed = nodes[first] + nodes[second]
        pair = merge * (weights[first] * weights[second]) * (summed * summed * summed)
        lost[first] = lost[first] + pair
        lost[second] = lost[second] + pair
        terms.append(pair)
        steps.append(jnp.exp(jnp.log(cubes[first] + cubes[second]) * (1.0 / 3.0)))
    for index in range(3):
        terms += [born[index], 2.0 * broken[index], -lost[index]]
        node = nodes[index]
        steps += [CUBE_ROOT_2 * node, (1.0 / CUBE_ROOT_2) * node, node]
    result = []
    for degree in range(MOMENTS):
        if degree:
            terms = [term * step for term, step in zip(terms, steps)]
        total = moment[degree]
        for term in terms:
            total = total + term
        result.append(total)
    return result


def kernel(
    moments_hbm,
    azimuth_hbm,
    radial_hbm,
    axial_hbm,
    shear_hbm,
    owner_hbm,
    target_hbm,
    weight_hbm,
    out_ref,
    cells,
    azimuth,
    radial,
    axial,
    shear,
    owner,
    target,
    weight,
    face,
    contrib,
    index_vmem,
    index_smem,
    outgoing,
    incoming,
    rim_out,
    rim_in,
    small_sem,
    cell_sem,
    weight_sem,
    send_sem,
    recv_sem,
    rim_send_sem,
    rim_recv_sem,
):
    region = lax.axis_index("region")
    me = lax.axis_index("cells")
    other = 1 - region
    after = lax.rem(me + 1, PEERS)
    before = lax.rem(me + PEERS - 1, PEERS)
    interface = (LAYERS - 1) * other
    per_chunk = ROWS // CHUNKS

    def plane(k, layer):
        return (k * (LAYERS + 2) + layer) * PLANE

    small = [
        pltpu.make_async_copy(owner_hbm, owner, small_sem.at[0]),
        pltpu.make_async_copy(target_hbm, target, small_sem.at[1]),
    ]
    for copy in small:
        copy.start()
    faces = [
        pltpu.make_async_copy(
            moments_hbm.at[k, interface], face.at[pl.ds(k * ROWS, ROWS)], cell_sem.at[k]
        )
        for k in range(MOMENTS)
    ]
    for copy in faces:
        copy.start()
    chunks = [
        pltpu.make_async_copy(
            weight_hbm.at[pl.ds(c * per_chunk * FACES, per_chunk * FACES)],
            weight.at[pl.ds(c * per_chunk * FACES, per_chunk * FACES)],
            weight_sem.at[c],
        )
        for c in range(CHUNKS)
    ]
    body_copies = []
    for k in range(MOMENTS):
        for layer in range(LAYERS):
            body_copies.append(
                pltpu.make_async_copy(
                    moments_hbm.at[k, layer],
                    cells.at[pl.ds(plane(k, layer + 1) + 8, ROWS)],
                    cell_sem.at[MOMENTS + k * LAYERS + layer],
                )
            )
    fields = [
        pltpu.make_async_copy(source, destination, small_sem.at[2 + i])
        for i, (source, destination) in enumerate(
            ((azimuth_hbm, azimuth), (radial_hbm, radial), (axial_hbm, axial), (shear_hbm, shear))
        )
    ]
    for c in range(CHUNKS - 2):
        chunks[c].start()
    for copy in body_copies:
        copy.start()
    for c in range(CHUNKS - 2, CHUNKS):
        chunks[c].start()
    for copy in fields:
        copy.start()

    barrier = pltpu.get_barrier_semaphore()

    def greet(peer, carry):
        pl.semaphore_signal(barrier, inc=1, device_id=(other, peer), device_id_type=MESH)
        return carry

    lax.fori_loop(0, PEERS, greet, 0, unroll=8)
    for peer in (after, before):
        pl.semaphore_signal(barrier, inc=1, device_id=(region, peer), device_id_type=MESH)

    for copy in small:
        copy.wait()
    square = (ROWS, PEERS)
    sublane = lax.broadcasted_iota(jnp.int32, square, 0)
    lane = lax.broadcasted_iota(jnp.int32, square, 1)
    by_lane = jnp.broadcast_to(owner[...], square)
    by_sublane = by_lane.T
    same = by_lane == by_sublane
    rank_row = jnp.sum(jnp.where(same & (sublane < lane), 1, 0), axis=0, keepdims=True)
    rank_column = jnp.sum(jnp.where(same & (lane < sublane), 1, 0), axis=1, keepdims=True)
    target_row = jnp.broadcast_to(target[...].astype(F32), square)
    meta = jnp.zeros(square, F32)
    index_vmem[...] = jnp.zeros(index_vmem.shape, jnp.int32)
    for r in range(SLOTS):
        chosen = (by_sublane == lane) & (rank_column == r)
        index = ROWS + jnp.sum(jnp.where(chosen, sublane - ROWS, 0), axis=0, keepdims=True)
        index_vmem[r : r + 1, :] = index
        chosen = (by_lane == sublane) & (rank_row == r)
        row = jnp.sum(jnp.where(chosen, target_row, 0.0), axis=1, keepdims=True)
        meta = jnp.where(lane == r, row, meta)
    outgoing[pl.ds(MESSAGE - 1, PEERS, stride=MESSAGE), :] = meta
    to_scalar = pltpu.make_async_copy(index_vmem, index_smem, small_sem.at[6])
    to_scalar.start()

    contrib[ROWS] = jnp.zeros((8, FACES), F32)
    for copy in faces:
        copy.wait()

    def weigh(z, carry):
        source = face[pl.ds(z, MOMENTS, stride=ROWS), :]
        source = jnp.concatenate([source, jnp.zeros((2, FACES), F32)], axis=0)
        source_high = source.astype(BF16).astype(F32)
        both = jnp.concatenate([source_high, source - source_high], axis=0).astype(BF16)
        matrix = weight[pl.ds(pl.multiple_of(z * FACES, FACES), FACES), :]
        high = matrix.astype(BF16)
        low = (matrix - high.astype(F32)).astype(BF16)
        product = lax.dot_general(
            both,
            jnp.concatenate([high, low], axis=0),
            (((1,), (1,)), ((), ())),
            preferred_element_type=F32,
        )
        contrib[z] = (
            product[:8, :FACES] + (product[8:, :FACES] + product[:8, FACES:])
        )
        return carry

    for c in range(CHUNKS - 2):
        chunks[c].wait()
        lax.fori_loop(c * per_chunk, (c + 1) * per_chunk, weigh, 0, unroll=4)

    for copy in body_copies:
        copy.wait()
    zero_rows = jnp.zeros((8, FACES), F32)

    def edges(i, carry):
        base = pl.multiple_of(i * PLANE, 8)
        cells[pl.ds(base, 8), :] = zero_rows
        cells[pl.ds(base + 8 + ROWS, 8), :] = zero_rows
        return carry

    lax.fori_loop(0, MOMENTS * (LAYERS + 2), edges, 0)
    for k in range(MOMENTS):
        empty = plane(k, (LAYERS + 1) * region)
        cells[pl.ds(empty + 8, ROWS), :] = jnp.zeros((ROWS, FACES), F32)

    lanes = lax.broadcasted_iota(jnp.int32, (8, FACES), 1)

    def pack(i, carry):
        packed = jnp.zeros((8, FACES), F32)
        for k in range(MOMENTS):
            for layer in range(LAYERS):
                p = k * LAYERS + layer
                values = cells[pl.ds(pl.multiple_of(plane(k, layer + 1) + 8 + i * 8, 8), 8), :]
                packed = jnp.where(lanes == p, pltpu.roll(values, p + 1, 1), packed)
        rim_out[pl.ds(pl.multiple_of(i * 8, 8), 8), :] = packed
        return carry

    lax.fori_loop(0, ROWS // 8, pack, 0)
    for c in range(CHUNKS - 2, CHUNKS):
        chunks[c].wait()
        lax.fori_loop(c * per_chunk, (c + 1) * per_chunk, weigh, 0, unroll=4)
    to_scalar.wait()

    pl.semaphore_wait(barrier, PEERS + 2)
    rim = pltpu.make_async_remote_copy(
        src_ref=rim_out,
        dst_ref=rim_in,
        send_sem=rim_send_sem,
        recv_sem=rim_recv_sem,
        device_id=(region, after),
        device_id_type=MESH,
    )
    rim.start()

    def dispatch(peer, carry):
        for r in range(SLOTS):
            block = index_smem[r, peer]
            values = contrib[block]
            outgoing[pl.ds(MESSAGE * peer + MOMENTS * r, MOMENTS), :] = values[:MOMENTS]
        pltpu.make_async_remote_copy(
            src_ref=outgoing.at[pl.ds(MESSAGE * peer, MESSAGE)],
            dst_ref=incoming.at[pl.ds(MESSAGE * me, MESSAGE)],
            send_sem=send_sem,
            recv_sem=recv_sem,
            device_id=(other, peer),
            device_id_type=MESH,
        ).start()
        return carry

    lax.fori_loop(0, PEERS, dispatch, 0, unroll=2)

    for copy in fields:
        copy.wait()
    rim.wait_recv()
    lanes_block = lax.broadcasted_iota(jnp.int32, (BLOCK, FACES), 1)

    def layer_step(layer, i):
        start = pl.multiple_of(i * BLOCK, BLOCK)
        at = pl.multiple_of(layer * ROWS + start, BLOCK)
        ca = azimuth[pl.ds(at, BLOCK), :]
        cr = radial[pl.ds(at, BLOCK), :]
        cz = axial[pl.ds(at, BLOCK), :]
        outward = cr > 0.0
        upward = cz > 0.0
        cr = jnp.abs(cr)
        cz = jnp.abs(cz)
        keep = 1.0 - ca - cr - cz
        rims = rim_in[pl.ds(start, BLOCK), :]
        advected = []
        for k in range(MOMENTS):
            row = plane(k, layer + 1) + 8 + start
            m = cells[pl.ds(row, BLOCK), :]
            shift = lax.rem(2 * FACES - (k * LAYERS + layer), FACES)
            previous = jnp.where(
                lanes_block == 0, pltpu.roll(rims, shift, 1), pltpu.roll(m, 1, 1)
            )
            below = cells[pl.ds(row - PLANE, BLOCK), :]
            beyond = cells[pl.ds(row + PLANE, BLOCK), :]
            axial_below = cells[pl.ds(row - 1, BLOCK), :]
            axial_beyond = cells[pl.ds(row + 1, BLOCK), :]
            advected.append(
                keep * m
                + ca * previous
                + cr * jnp.where(outward, below, beyond)
                + cz * jnp.where(upward, axial_below, axial_beyond)
            )
        result = sources(advected, shear[pl.ds(at, BLOCK), :])
        for k in range(MOMENTS):
            out_ref[k, layer, pl.ds(start, BLOCK), :] = result[k]

    def inner(n, carry):
        layer = region + n // (ROWS // BLOCK)
        layer_step(layer, lax.rem(n, ROWS // BLOCK))
        return carry

    lax.fori_loop(0, (LAYERS - 1) * (ROWS // BLOCK), inner, 0)

    whole = pltpu.make_async_remote_copy(
        src_ref=outgoing,
        dst_ref=incoming,
        send_sem=send_sem,
        recv_sem=recv_sem,
        device_id=(other, me),
        device_id_type=MESH,
    )
    whole.wait_recv()

    meta = incoming[pl.ds(MESSAGE - 1, PEERS, stride=MESSAGE), :]
    hits = jnp.concatenate(
        [jnp.where(meta[:, r : r + 1] == lane.astype(F32), 1.0, 0.0).T for r in range(SLOTS)], axis=1
    ).astype(BF16)
    ghost_layer = (LAYERS + 1) * other
    for k in range(MOMENTS):
        received = jnp.concatenate(
            [
                incoming[pl.ds(r * MOMENTS + k, PEERS, stride=MESSAGE), :]
                for r in range(SLOTS)
            ],
            axis=0,
        )
        high = received.astype(BF16)
        low = (received - high.astype(F32)).astype(BF16)
        summed = jnp.dot(
            hits, jnp.concatenate([high, low], axis=1), preferred_element_type=F32
        )
        cells[pl.ds(plane(k, ghost_layer) + 8, ROWS), :] = summed[:, :FACES] + summed[:, FACES:]

    def outer(i, carry):
        layer_step(interface, i)
        return carry

    lax.fori_loop(0, ROWS // BLOCK, outer, 0)
    whole.wait_send()
    rim.wait_send()


def on_device(
    moments, courant_azimuth, courant_radial, courant_axial, shear, owner, target, ami_weight
):
    shape = (MOMENTS, LAYERS, ROWS, FACES)
    field = (LAYERS * ROWS, FACES)
    dma = pltpu.SemaphoreType.DMA
    updated = pl.pallas_call(
        kernel,
        out_shape=jax.ShapeDtypeStruct(shape, F32),
        in_specs=[pl.BlockSpec(memory_space=pl.ANY)] * 8,
        out_specs=pl.BlockSpec(memory_space=pltpu.VMEM),
        scratch_shapes=[
            pltpu.VMEM((MOMENTS * (LAYERS + 2) * PLANE, FACES), F32),
            pltpu.VMEM(field, F32),
            pltpu.VMEM(field, F32),
            pltpu.VMEM(field, F32),
            pltpu.VMEM(field, F32),
            pltpu.VMEM((1, ROWS), jnp.int32),
            pltpu.VMEM((1, ROWS), jnp.int32),
            pltpu.VMEM((ROWS * FACES, FACES), F32),
            pltpu.VMEM((MOMENTS * ROWS, FACES), F32),
            pltpu.VMEM((ROWS + 1, 8, FACES), F32),
            pltpu.VMEM((8, PEERS), jnp.int32),
            pltpu.SMEM((8, PEERS), jnp.int32),
            pltpu.VMEM((MESSAGE * PEERS, FACES), F32),
            pltpu.VMEM((MESSAGE * PEERS, FACES), F32),
            pltpu.VMEM((ROWS, FACES), F32),
            pltpu.VMEM((ROWS, FACES), F32),
            dma((7,)),
            dma((MOMENTS + MOMENTS * LAYERS,)),
            dma((CHUNKS,)),
            dma,
            dma,
            dma,
            dma,
        ],
        compiler_params=pltpu.CompilerParams(
            collective_id=0, has_side_effects=True, vmem_limit_bytes=48 * 1024 * 1024
        ),
        name="transport",
    )(
        moments.reshape(shape),
        courant_azimuth.reshape(field),
        courant_radial.reshape(field),
        courant_axial.reshape(field),
        shear.reshape(field),
        owner.reshape(1, ROWS),
        target.reshape(1, ROWS),
        ami_weight.reshape(ROWS * FACES, FACES),
    )
    return updated[None]


def solution(mesh):
    placed = (
        P("region", None, None, None, "cells"),
        P("region", None, None, "cells"),
        P("region", None, None, "cells"),
        P("region", None, None, "cells"),
        P("region", None, None, "cells"),
        P("region", "cells", None),
        P("region", "cells"),
        P("region", "cells", None, None),
    )
    return jax.shard_map(
        on_device,
        mesh=mesh,
        in_specs=placed,
        out_specs=P("region", None, None, None, "cells"),
        check_vma=False,
    )
```

time: 99.6 us -> 51.1 us (0.51)
  the two profiles are of different devices: /device:TPU:1 before, /device:TPU:65 now
where the time goes in v1:
time: 51.1 us; the launch traced here: 50.8 us
  Pallas kernels  43.1 us (84%)
  local copies, waits for them, and re-layouts  7.66 us (15%)
    pallas_call x1, Pallas kernels, on_device(): pl.pallas_call(kernel, out_shape=jax.ShapeDtypeStruct(shape, F32), in_spe...  43.1 us
    unnamed x15, local copies, waits for them, and re-layouts  7.66 us

profile of v1, /device:TPU:65, one launch (start us, length us, event | category | flops | bytes accessed | tf_op | source)
XLA Modules:
  0.0 50.8 jit_solution(8221961722541829719)
XLA Ops:
  0.0 0.0 copy-start
  0.0 1.4 %copy-done = f32[1,6,4,128,128]{4,3,2,1,0:T(8,128)S(1)} copy-done((f32[1,6,4,128,128]{4,3,2,1,0:T(8,128)S(1)}, f32[1,6,4,128,128]{4,3,2,1,0:T(8,128)}, u32[]{:S(2)}) %copy-start) | copy-done | bytes 1572888
  1.4 0.0 copy-start.1
  1.4 0.9 %copy-done.1 = f32[1,4,128,128]{3,2,1,0:T(8,128)S(1)} copy-done((f32[1,4,128,128]{3,2,1,0:T(8,128)S(1)}, f32[1,4,128,128]{3,2,1,0:T(8,128)}, u32[]{:S(2)}) %copy-start.1) | copy-done | bytes 262168
  2.4 0.0 copy-start.2
  2.4 0.9 %copy-done.2 = f32[1,4,128,128]{3,2,1,0:T(8,128)S(1)} copy-done((f32[1,4,128,128]{3,2,1,0:T(8,128)S(1)}, f32[1,4,128,128]{3,2,1,0:T(8,128)}, u32[]{:S(2)}) %copy-start.2) | copy-done | bytes 262168
  3.3 0.0 copy-start.3
  3.3 0.9 %copy-done.3 = f32[1,4,128,128]{3,2,1,0:T(8,128)S(1)} copy-done((f32[1,4,128,128]{3,2,1,0:T(8,128)S(1)}, f32[1,4,128,128]{3,2,1,0:T(8,128)}, u32[]{:S(2)}) %copy-start.3) | copy-done | bytes 262168
  4.3 0.0 copy-start.4
  4.3 0.9 %copy-done.4 = f32[1,4,128,128]{3,2,1,0:T(8,128)S(1)} copy-done((f32[1,4,128,128]{3,2,1,0:T(8,128)S(1)}, f32[1,4,128,128]{3,2,1,0:T(8,128)}, u32[]{:S(2)}) %copy-start.4) | copy-done | bytes 262168
  5.2 0.0 copy-start.5
  5.2 0.7 %copy-done.5 = s32[1,128,1]{1,2,0:T(1,128)S(1)} copy-done((s32[1,128,1]{1,2,0:T(1,128)S(1)}, s32[1,128,1]{1,2,0:T(1,128)}, u32[]{:S(2)}) %copy-start.5) | copy-done | bytes 536
  5.9 0.0 copy-start.6
  5.9 0.7 %copy-done.6 = s32[1,128]{1,0:T(1,128)S(1)} copy-done((s32[1,128]{1,0:T(1,128)S(1)}, s32[1,128]{1,0:T(1,128)}, u32[]{:S(2)}) %copy-start.6) | copy-done | bytes 536
  6.5 43.1 %transport.1 = f32[6,4,128,128]{3,2,1,0:T(8,128)S(1)} custom-call(f32[6,4,128,128]{3,2,1,0:T(8,128)S(1)} %bitcast.9, f32[512,128]{1,0:T(8,128)S(1)} %bitcast.10, f32[512,128]{1,0:T(8,128)S(1)} %bitcast.11, f32[512,128]{1,0:T(8,128)S(1)} %bitcast.12, f32[512,128]{1,0:T(8,128)S(1)} %bitcast.13, s32[1,128]{1,0:T(1,128)S(1)} %bitcast.14, ...), custom_call_target="tpu_custom_call" | custom-call | tf_op jit(solution)/shard_map/transport/pallas_call | solution.py:422
  49.7 1.1 %copy.10 = f32[1,6,4,128,128]{4,3,2,1,0:T(8,128)} copy(f32[1,6,4,128,128]{4,3,2,1,0:T(8,128)S(1)} %bitcast.8) | data formatting | bytes 3145728
Async XLA Ops:
  0.0 1.4 %copy-start = (f32[1,6,4,128,128]{4,3,2,1,0:T(8,128)S(1)}, f32[1,6,4,128,128]{4,3,2,1,0:T(8,128)}, u32[]{:S(2)}) copy-start(f32[1,6,4,128,128]{4,3,2,1,0:T(8,128)} %param.8) | copy-start | bytes 4718596
  1.4 0.9 %copy-start.1 = (f32[1,4,128,128]{3,2,1,0:T(8,128)S(1)}, f32[1,4,128,128]{3,2,1,0:T(8,128)}, u32[]{:S(2)}) copy-start(f32[1,4,128,128]{3,2,1,0:T(8,128)} %param.9) | copy-start | bytes 786436
  2.4 0.9 %copy-start.2 = (f32[1,4,128,128]{3,2,1,0:T(8,128)S(1)}, f32[1,4,128,128]{3,2,1,0:T(8,128)}, u32[]{:S(2)}) copy-start(f32[1,4,128,128]{3,2,1,0:T(8,128)} %param.10) | copy-start | bytes 786436
  3.3 0.9 %copy-start.3 = (f32[1,4,128,128]{3,2,1,0:T(8,128)S(1)}, f32[1,4,128,128]{3,2,1,0:T(8,128)}, u32[]{:S(2)}) copy-start(f32[1,4,128,128]{3,2,1,0:T(8,128)} %param.11) | copy-start | bytes 786436
  4.3 0.9 %copy-start.4 = (f32[1,4,128,128]{3,2,1,0:T(8,128)S(1)}, f32[1,4,128,128]{3,2,1,0:T(8,128)}, u32[]{:S(2)}) copy-start(f32[1,4,128,128]{3,2,1,0:T(8,128)} %param.12) | copy-start | bytes 786436
  5.2 0.7 %copy-start.5 = (s32[1,128,1]{1,2,0:T(1,128)S(1)}, s32[1,128,1]{1,2,0:T(1,128)}, u32[]{:S(2)}) copy-start(s32[1,128,1]{1,2,0:T(1,128)} %param.13) | copy-start | bytes 1540
  5.9 0.7 %copy-start.6 = (s32[1,128]{1,0:T(1,128)S(1)}, s32[1,128]{1,0:T(1,128)}, u32[]{:S(2)}) copy-start(s32[1,128]{1,0:T(1,128)} %target_hbm.1) | copy-start | bytes 1540

commit v2 on v1

--- a/solution.py
+++ b/solution.py
@@ -265,7 +265,7 @@
 
     for c in range(CHUNKS - 2):
         chunks[c].wait()
-        lax.fori_loop(c * per_chunk, (c + 1) * per_chunk, weigh, 0, unroll=4)
+        lax.fori_loop(c * per_chunk, (c + 1) * per_chunk, weigh, 0, unroll=per_chunk)
 
     for copy in body_copies:
         copy.wait()
@@ -297,7 +297,7 @@
     lax.fori_loop(0, ROWS // 8, pack, 0)
     for c in range(CHUNKS - 2, CHUNKS):
         chunks[c].wait()
-        lax.fori_loop(c * per_chunk, (c + 1) * per_chunk, weigh, 0, unroll=4)
+        lax.fori_loop(c * per_chunk, (c + 1) * per_chunk, weigh, 0, unroll=per_chunk)
     to_scalar.wait()
 
     pl.semaphore_wait(barrier, PEERS + 2)
@@ -422,7 +422,7 @@
     updated = pl.pallas_call(
         kernel,
         out_shape=jax.ShapeDtypeStruct(shape, F32),
-        in_specs=[pl.BlockSpec(memory_space=pl.ANY)] * 8,
+        in_specs=[pl.BlockSpec(memory_space=pltpu.HBM)] * 8,
         out_specs=pl.BlockSpec(memory_space=pltpu.VMEM),
         scratch_shapes=[
             pltpu.VMEM((MOMENTS * (LAYERS + 2) * PLANE, FACES), F32),
@@ -454,14 +454,19 @@
         ),
         name="transport",
     )(
-        moments.reshape(shape),
-        courant_azimuth.reshape(field),
-        courant_radial.reshape(field),
-        courant_axial.reshape(field),
-        shear.reshape(field),
-        owner.reshape(1, ROWS),
-        target.reshape(1, ROWS),
-        ami_weight.reshape(ROWS * FACES, FACES),
+        *[
+            pltpu.with_memory_space_constraint(operand, pltpu.HBM)
+            for operand in (
+                moments.reshape(shape),
+                courant_azimuth.reshape(field),
+                courant_radial.reshape(field),
+                courant_axial.reshape(field),
+                shear.reshape(field),
+                owner.reshape(1, ROWS),
+                target.reshape(1, ROWS),
+                ami_weight.reshape(ROWS * FACES, FACES),
+            )
+        ]
     )
     return updated[None]
 

time: 51.1 us -> 39.9 us (0.78)
  local copies, waits for them, and re-layouts: 7.66 us -> 1.15 us
  Pallas kernels: 43.1 us -> 38.7 us
    unnamed x15 -> x1, local copies, waits for them, and re-layouts: 7.66 us -> 1.15 us
    pallas_call x1, Pallas kernels: 43.1 us -> 38.7 us  [on_device(): pl.pallas_call(kernel, out_shape=jax.ShapeDtypeStruct(shape, F32), in_spe...]
where the time goes in v2:
time: 39.9 us
  Pallas kernels  38.7 us (97%)
  local copies, waits for them, and re-layouts  1.15 us (3%)
    pallas_call x1, Pallas kernels, on_device(): pl.pallas_call(kernel, out_shape=jax.ShapeDtypeStruct(shape, F32), in_spe...  38.7 us
    unnamed x1, local copies, waits for them, and re-layouts  1.15 us

profile of v2, /device:TPU:65, one launch (start us, length us, event | category | flops | bytes accessed | tf_op | source)
XLA Modules:
  0.0 39.9 jit_solution(17604836703514549722)
XLA Ops:
  0.0 38.7 %transport.1 = f32[6,4,128,128]{3,2,1,0:T(8,128)S(1)} custom-call(f32[6,4,128,128]{3,2,1,0:T(8,128)} %bitcast.10, f32[512,128]{1,0:T(8,128)} %bitcast.11, f32[512,128]{1,0:T(8,128)} %bitcast.12, f32[512,128]{1,0:T(8,128)} %bitcast.13, f32[512,128]{1,0:T(8,128)} %bitcast.14, s32[1,128]{1,0:T(1,128)} %bitcast.15, s32[1,128]{1,0:T(1,128)} %target_hbm.1, ...), custom_call_target="tpu_custom_call" | custom-call | tf_op jit(solution)/shard_map/transport/pallas_call | solution.py:422
  38.7 1.1 %copy.10 = f32[1,6,4,128,128]{4,3,2,1,0:T(8,128)} copy(f32[1,6,4,128,128]{4,3,2,1,0:T(8,128)S(1)} %bitcast.8) | data formatting | bytes 3145728

commit v3 on v2

--- a/solution.py
+++ b/solution.py
@@ -18,10 +18,13 @@
 MOMENTS = 6
 PEERS = 128
 SLOTS = 2
-MESSAGE = SLOTS * MOMENTS + 1
+MESSAGE = SLOTS * MOMENTS
+DEPTH = 8
+FLAT = PEERS // DEPTH
 PLANE = ROWS + 16
 CHUNKS = 8
-BLOCK = 16
+EARLY = 32
+BLOCK = 32
 CUBE_ROOT_2 = 2.0 ** (1.0 / 3.0)
 
 THIRD_ANGLE = (
@@ -140,6 +143,10 @@
     incoming,
     rim_out,
     rim_in,
+    rows_out,
+    rows_in,
+    partial,
+    ghost_weight,
     small_sem,
     cell_sem,
     weight_sem,
@@ -147,6 +154,10 @@
     recv_sem,
     rim_send_sem,
     rim_recv_sem,
+    hop_send_sem,
+    hop_recv_sem,
+    rows_send_sem,
+    rows_recv_sem,
 ):
     region = lax.axis_index("region")
     me = lax.axis_index("cells")
@@ -154,6 +165,8 @@
     after = lax.rem(me + 1, PEERS)
     before = lax.rem(me + PEERS - 1, PEERS)
     interface = (LAYERS - 1) * other
+    depth, flat = me // FLAT, lax.rem(me, FLAT)
+    place = flat * DEPTH + depth
     per_chunk = ROWS // CHUNKS
 
     def plane(k, layer):
@@ -197,13 +210,7 @@
             ((azimuth_hbm, azimuth), (radial_hbm, radial), (axial_hbm, axial), (shear_hbm, shear))
         )
     ]
-    for c in range(CHUNKS - 2):
-        chunks[c].start()
-    for copy in body_copies:
-        copy.start()
-    for c in range(CHUNKS - 2, CHUNKS):
-        chunks[c].start()
-    for copy in fields:
+    for copy in chunks + body_copies:
         copy.start()
 
     barrier = pltpu.get_barrier_semaphore()
@@ -213,7 +220,9 @@
         return carry
 
     lax.fori_loop(0, PEERS, greet, 0, unroll=8)
-    for peer in (after, before):
+    column = [lax.rem(depth + i, DEPTH) * FLAT + flat for i in range(1, DEPTH)]
+    near = [after, before] + column
+    for peer in near:
         pl.semaphore_signal(barrier, inc=1, device_id=(region, peer), device_id_type=MESH)
 
     for copy in small:
@@ -224,19 +233,15 @@
     by_lane = jnp.broadcast_to(owner[...], square)
     by_sublane = by_lane.T
     same = by_lane == by_sublane
-    rank_row = jnp.sum(jnp.where(same & (sublane < lane), 1, 0), axis=0, keepdims=True)
-    rank_column = jnp.sum(jnp.where(same & (lane < sublane), 1, 0), axis=1, keepdims=True)
-    target_row = jnp.broadcast_to(target[...].astype(F32), square)
-    meta = jnp.zeros(square, F32)
+    rank = jnp.sum(jnp.where(same & (lane < sublane), 1, 0), axis=1, keepdims=True)
+    target_column = jnp.broadcast_to(target[...], square).T
     index_vmem[...] = jnp.zeros(index_vmem.shape, jnp.int32)
     for r in range(SLOTS):
-        chosen = (by_sublane == lane) & (rank_column == r)
+        chosen = (by_sublane == lane) & (rank == r)
         index = ROWS + jnp.sum(jnp.where(chosen, sublane - ROWS, 0), axis=0, keepdims=True)
         index_vmem[r : r + 1, :] = index
-        chosen = (by_lane == sublane) & (rank_row == r)
-        row = jnp.sum(jnp.where(chosen, target_row, 0.0), axis=1, keepdims=True)
-        meta = jnp.where(lane == r, row, meta)
-    outgoing[pl.ds(MESSAGE - 1, PEERS, stride=MESSAGE), :] = meta
+        row = jnp.sum(jnp.where(chosen, target_column, 0), axis=0, keepdims=True)
+        rows_out[pl.ds(r * DEPTH + depth, 1), :] = row
     to_scalar = pltpu.make_async_copy(index_vmem, index_smem, small_sem.at[6])
     to_scalar.start()
 
@@ -263,25 +268,45 @@
         )
         return carry
 
-    for c in range(CHUNKS - 2):
+    for c in range(CHUNKS):
         chunks[c].wait()
         lax.fori_loop(c * per_chunk, (c + 1) * per_chunk, weigh, 0, unroll=per_chunk)
+    for copy in fields:
+        copy.start()
+    to_scalar.wait()
+
+    pl.semaphore_wait(barrier, PEERS + len(near))
+
+    for peer in column:
+        for r in range(SLOTS):
+            row = rows_out.at[pl.ds(r * DEPTH + depth, 1)]
+            pltpu.make_async_remote_copy(
+                src_ref=row,
+                dst_ref=row,
+                send_sem=hop_send_sem,
+                recv_sem=hop_recv_sem,
+                device_id=(region, peer),
+                device_id_type=MESH,
+            ).start()
+
+    def dispatch(peer, carry):
+        for r in range(SLOTS):
+            block = index_smem[r, peer]
+            values = contrib[block]
+            outgoing[pl.ds(MESSAGE * peer + MOMENTS * r, MOMENTS), :] = values[:MOMENTS]
+        pltpu.make_async_remote_copy(
+            src_ref=outgoing.at[pl.ds(MESSAGE * peer, MESSAGE)],
+            dst_ref=incoming.at[pl.ds(MESSAGE * place, MESSAGE)],
+            send_sem=send_sem,
+            recv_sem=recv_sem,
+            device_id=(other, peer),
+            device_id_type=MESH,
+        ).start()
+        return carry
+
 
     for copy in body_copies:
         copy.wait()
-    zero_rows = jnp.zeros((8, FACES), F32)
-
-    def edges(i, carry):
-        base = pl.multiple_of(i * PLANE, 8)
-        cells[pl.ds(base, 8), :] = zero_rows
-        cells[pl.ds(base + 8 + ROWS, 8), :] = zero_rows
-        return carry
-
-    lax.fori_loop(0, MOMENTS * (LAYERS + 2), edges, 0)
-    for k in range(MOMENTS):
-        empty = plane(k, (LAYERS + 1) * region)
-        cells[pl.ds(empty + 8, ROWS), :] = jnp.zeros((ROWS, FACES), F32)
-
     lanes = lax.broadcasted_iota(jnp.int32, (8, FACES), 1)
 
     def pack(i, carry):
@@ -295,12 +320,6 @@
         return carry
 
     lax.fori_loop(0, ROWS // 8, pack, 0)
-    for c in range(CHUNKS - 2, CHUNKS):
-        chunks[c].wait()
-        lax.fori_loop(c * per_chunk, (c + 1) * per_chunk, weigh, 0, unroll=per_chunk)
-    to_scalar.wait()
-
-    pl.semaphore_wait(barrier, PEERS + 2)
     rim = pltpu.make_async_remote_copy(
         src_ref=rim_out,
         dst_ref=rim_in,
@@ -311,29 +330,51 @@
     )
     rim.start()
 
-    def dispatch(peer, carry):
+    lax.fori_loop(0, PEERS, dispatch, 0, unroll=2)
+
+    hop = pltpu.make_async_remote_copy(
+        src_ref=rows_out.at[pl.ds(0, SLOTS * (DEPTH - 1))],
+        dst_ref=rows_out.at[pl.ds(0, SLOTS * (DEPTH - 1))],
+        send_sem=hop_send_sem,
+        recv_sem=hop_recv_sem,
+        device_id=(region, after),
+        device_id_type=MESH,
+    )
+    hop.wait_recv()
+
+    def spread(i, carry):
         for r in range(SLOTS):
-            block = index_smem[r, peer]
-            values = contrib[block]
-            outgoing[pl.ds(MESSAGE * peer + MOMENTS * r, MOMENTS), :] = values[:MOMENTS]
-        pltpu.make_async_remote_copy(
-            src_ref=outgoing.at[pl.ds(MESSAGE * peer, MESSAGE)],
-            dst_ref=incoming.at[pl.ds(MESSAGE * me, MESSAGE)],
-            send_sem=send_sem,
-            recv_sem=recv_sem,
-            device_id=(other, peer),
-            device_id_type=MESH,
-        ).start()
-        return carry
-
-    lax.fori_loop(0, PEERS, dispatch, 0, unroll=2)
+            pltpu.make_async_remote_copy(
+                src_ref=rows_out.at[pl.ds(r * DEPTH, DEPTH)],
+                dst_ref=rows_in.at[pl.ds(r * PEERS + flat * DEPTH, DEPTH)],
+                send_sem=rows_send_sem,
+                recv_sem=rows_recv_sem,
+                device_id=(other, depth * FLAT + i),
+                device_id_type=MESH,
+            ).start()
+        return carry
+
+    lax.fori_loop(0, FLAT, spread, 0)
+
+    zero_rows = jnp.zeros((8, FACES), F32)
+
+    def edges(i, carry):
+        base = pl.multiple_of(i * PLANE, 8)
+        cells[pl.ds(base, 8), :] = zero_rows
+        cells[pl.ds(base + 8 + ROWS, 8), :] = zero_rows
+        return carry
+
+    lax.fori_loop(0, MOMENTS * (LAYERS + 2), edges, 0)
+    for k in range(MOMENTS):
+        empty = plane(k, (LAYERS + 1) * region)
+        cells[pl.ds(empty + 8, ROWS), :] = jnp.zeros((ROWS, FACES), F32)
 
     for copy in fields:
         copy.wait()
     rim.wait_recv()
     lanes_block = lax.broadcasted_iota(jnp.int32, (BLOCK, FACES), 1)
 
-    def layer_step(layer, i):
+    def advect(layer, i, at_interface):
         start = pl.multiple_of(i * BLOCK, BLOCK)
         at = pl.multiple_of(layer * ROWS + start, BLOCK)
         ca = azimuth[pl.ds(at, BLOCK), :]
@@ -345,6 +386,10 @@
         cz = jnp.abs(cz)
         keep = 1.0 - ca - cr - cz
         rims = rim_in[pl.ds(start, BLOCK), :]
+        if at_interface:
+            from_ghost = outward == (region == 1)
+            ghost_weight[pl.ds(start, BLOCK), :] = jnp.where(from_ghost, cr, 0.0)
+            cr = jnp.where(from_ghost, 0.0, cr)
         advected = []
         for k in range(MOMENTS):
             row = plane(k, layer + 1) + 8 + start
@@ -353,26 +398,60 @@
             previous = jnp.where(
                 lanes_block == 0, pltpu.roll(rims, shift, 1), pltpu.roll(m, 1, 1)
             )
-            below = cells[pl.ds(row - PLANE, BLOCK), :]
-            beyond = cells[pl.ds(row + PLANE, BLOCK), :]
             axial_below = cells[pl.ds(row - 1, BLOCK), :]
             axial_beyond = cells[pl.ds(row + 1, BLOCK), :]
+            if at_interface:
+                radial_side = cells[pl.ds(row + (2 * region - 1) * PLANE, BLOCK), :]
+            else:
+                below = cells[pl.ds(row - PLANE, BLOCK), :]
+                beyond = cells[pl.ds(row + PLANE, BLOCK), :]
+                radial_side = jnp.where(outward, below, beyond)
             advected.append(
                 keep * m
                 + ca * previous
-                + cr * jnp.where(outward, below, beyond)
+                + cr * radial_side
                 + cz * jnp.where(upward, axial_below, axial_beyond)
             )
+        return advected
+
+    def finish(layer, i, advected):
+        start = pl.multiple_of(i * BLOCK, BLOCK)
+        at = pl.multiple_of(layer * ROWS + start, BLOCK)
         result = sources(advected, shear[pl.ds(at, BLOCK), :])
         for k in range(MOMENTS):
             out_ref[k, layer, pl.ds(start, BLOCK), :] = result[k]
 
     def inner(n, carry):
         layer = region + n // (ROWS // BLOCK)
-        layer_step(layer, lax.rem(n, ROWS // BLOCK))
+        i = lax.rem(n, ROWS // BLOCK)
+        finish(layer, i, advect(layer, i, False))
         return carry
 
     lax.fori_loop(0, (LAYERS - 1) * (ROWS // BLOCK), inner, 0)
+
+    def prepare(i, carry):
+        advected = advect(interface, i, True)
+        for k in range(MOMENTS):
+            partial[pl.ds(pl.multiple_of(k * ROWS + i * BLOCK, BLOCK), BLOCK), :] = advected[k]
+        return carry
+
+    lax.fori_loop(0, ROWS // BLOCK, prepare, 0)
+
+    rows = pltpu.make_async_remote_copy(
+        src_ref=rows_in,
+        dst_ref=rows_in,
+        send_sem=rows_send_sem,
+        recv_sem=rows_recv_sem,
+        device_id=(other, me),
+        device_id_type=MESH,
+    )
+    rows.wait_recv()
+    mine = []
+    for r in range(SLOTS):
+        named = jnp.where(lane == me, rows_in[pl.ds(r * PEERS, PEERS), :], 0)
+        named = jnp.sum(named, axis=1, keepdims=True)
+        mine.append(jnp.where(named == lane, 1.0, 0.0).T)
+    hits = jnp.concatenate(mine, axis=1).astype(BF16)
 
     whole = pltpu.make_async_remote_copy(
         src_ref=outgoing,
@@ -384,11 +463,6 @@
     )
     whole.wait_recv()
 
-    meta = incoming[pl.ds(MESSAGE - 1, PEERS, stride=MESSAGE), :]
-    hits = jnp.concatenate(
-        [jnp.where(meta[:, r : r + 1] == lane.astype(F32), 1.0, 0.0).T for r in range(SLOTS)], axis=1
-    ).astype(BF16)
-    ghost_layer = (LAYERS + 1) * other
     for k in range(MOMENTS):
         received = jnp.concatenate(
             [
@@ -402,15 +476,23 @@
         summed = jnp.dot(
             hits, jnp.concatenate([high, low], axis=1), preferred_element_type=F32
         )
-        cells[pl.ds(plane(k, ghost_layer) + 8, ROWS), :] = summed[:, :FACES] + summed[:, FACES:]
+        ghost = summed[:, :FACES] + summed[:, FACES:]
+        at = pl.ds(k * ROWS, ROWS)
+        partial[at, :] = partial[at, :] + ghost_weight[...] * ghost
 
     def outer(i, carry):
-        layer_step(interface, i)
+        advected = [
+            partial[pl.ds(pl.multiple_of(k * ROWS + i * BLOCK, BLOCK), BLOCK), :]
+            for k in range(MOMENTS)
+        ]
+        finish(interface, i, advected)
         return carry
 
     lax.fori_loop(0, ROWS // BLOCK, outer, 0)
     whole.wait_send()
     rim.wait_send()
+    hop.wait_send()
+    rows.wait_send()
 
 
 def on_device(
@@ -441,9 +523,17 @@
             pltpu.VMEM((MESSAGE * PEERS, FACES), F32),
             pltpu.VMEM((ROWS, FACES), F32),
             pltpu.VMEM((ROWS, FACES), F32),
+            pltpu.VMEM((SLOTS * DEPTH, PEERS), jnp.int32),
+            pltpu.VMEM((SLOTS * PEERS, PEERS), jnp.int32),
+            pltpu.VMEM((MOMENTS * ROWS, FACES), F32),
+            pltpu.VMEM((ROWS, FACES), F32),
             dma((7,)),
             dma((MOMENTS + MOMENTS * LAYERS,)),
             dma((CHUNKS,)),
+            dma,
+            dma,
+            dma,
+            dma,
             dma,
             dma,
             dma,

time: 39.9 us -> 38.8 us (0.972)
  Pallas kernels: 38.7 us -> 37.5 us
    pallas_call x1, Pallas kernels: 38.7 us -> 37.5 us  [on_device(): pl.pallas_call(kernel, out_shape=jax.ShapeDtypeStruct(shape, F32), in_spe...]
where the time goes in v3:
time: 38.8 us; the launch traced here: 38.7 us
  Pallas kernels  37.5 us (97%)
  local copies, waits for them, and re-layouts  1.15 us (3%)
    pallas_call x1, Pallas kernels, on_device(): pl.pallas_call(kernel, out_shape=jax.ShapeDtypeStruct(shape, F32), in_spe...  37.5 us
    unnamed x1, local copies, waits for them, and re-layouts  1.15 us

profile of v3, /device:TPU:65, one launch (start us, length us, event | category | flops | bytes accessed | tf_op | source)
XLA Modules:
  0.0 38.7 jit_solution(14841898257158251588)
XLA Ops:
  0.0 37.5 %transport.1 = f32[6,4,128,128]{3,2,1,0:T(8,128)S(1)} custom-call(f32[6,4,128,128]{3,2,1,0:T(8,128)} %bitcast.10, f32[512,128]{1,0:T(8,128)} %bitcast.11, f32[512,128]{1,0:T(8,128)} %bitcast.12, f32[512,128]{1,0:T(8,128)} %bitcast.13, f32[512,128]{1,0:T(8,128)} %bitcast.14, s32[1,128]{1,0:T(1,128)} %bitcast.15, s32[1,128]{1,0:T(1,128)} %target_hbm.1, ...), custom_call_target="tpu_custom_call" | custom-call | tf_op jit(solution)/shard_map/transport/pallas_call | solution.py:504
  37.5 1.1 %copy.10 = f32[1,6,4,128,128]{4,3,2,1,0:T(8,128)} copy(f32[1,6,4,128,128]{4,3,2,1,0:T(8,128)S(1)} %bitcast.8) | data formatting | bytes 3145728

commit v4 on v3

--- a/solution.py
+++ b/solution.py
@@ -210,7 +210,7 @@
             ((azimuth_hbm, azimuth), (radial_hbm, radial), (axial_hbm, axial), (shear_hbm, shear))
         )
     ]
-    for copy in chunks + body_copies:
+    for copy in chunks + body_copies + fields:
         copy.start()
 
     barrier = pltpu.get_barrier_semaphore()
@@ -271,8 +271,6 @@
     for c in range(CHUNKS):
         chunks[c].wait()
         lax.fori_loop(c * per_chunk, (c + 1) * per_chunk, weigh, 0, unroll=per_chunk)
-    for copy in fields:
-        copy.start()
     to_scalar.wait()
 
     pl.semaphore_wait(barrier, PEERS + len(near))
@@ -319,7 +317,7 @@
         rim_out[pl.ds(pl.multiple_of(i * 8, 8), 8), :] = packed
         return carry
 
-    lax.fori_loop(0, ROWS // 8, pack, 0)
+    lax.fori_loop(0, ROWS // 8, pack, 0, unroll=4)
     rim = pltpu.make_async_remote_copy(
         src_ref=rim_out,
         dst_ref=rim_in,

time: 38.8 us -> 36.7 us (0.946)
  Pallas kernels: 37.5 us -> 35.5 us
    pallas_call x1, Pallas kernels: 37.5 us -> 35.5 us  [on_device(): pl.pallas_call(kernel, out_shape=jax.ShapeDtypeStruct(shape, F32), in_spe...]
where the time goes in v4:
time: 36.7 us; the launch traced here: 36.6 us
  Pallas kernels  35.5 us (97%)
  local copies, waits for them, and re-layouts  1.15 us (3%)
    pallas_call x1, Pallas kernels, on_device(): pl.pallas_call(kernel, out_shape=jax.ShapeDtypeStruct(shape, F32), in_spe...  35.5 us
    unnamed x1, local copies, waits for them, and re-layouts  1.15 us

profile of v4, /device:TPU:65, one launch (start us, length us, event | category | flops | bytes accessed | tf_op | source)
XLA Modules:
  0.0 36.6 jit_solution(18343559830386245114)
XLA Ops:
  0.0 35.5 %transport.1 = f32[6,4,128,128]{3,2,1,0:T(8,128)S(1)} custom-call(f32[6,4,128,128]{3,2,1,0:T(8,128)} %bitcast.10, f32[512,128]{1,0:T(8,128)} %bitcast.11, f32[512,128]{1,0:T(8,128)} %bitcast.12, f32[512,128]{1,0:T(8,128)} %bitcast.13, f32[512,128]{1,0:T(8,128)} %bitcast.14, s32[1,128]{1,0:T(1,128)} %bitcast.15, s32[1,128]{1,0:T(1,128)} %target_hbm.1, ...), custom_call_target="tpu_custom_call" | custom-call | tf_op jit(solution)/shard_map/transport/pallas_call | solution.py:502
  35.5 1.1 %copy.10 = f32[1,6,4,128,128]{4,3,2,1,0:T(8,128)} copy(f32[1,6,4,128,128]{4,3,2,1,0:T(8,128)S(1)} %bitcast.8) | data formatting | bytes 3145728

commit v5 on v4

--- a/solution.py
+++ b/solution.py
@@ -18,11 +18,11 @@
 MOMENTS = 6
 PEERS = 128
 SLOTS = 2
+PLANES = MOMENTS * LAYERS
 MESSAGE = SLOTS * MOMENTS
 DEPTH = 8
 FLAT = PEERS // DEPTH
-PLANE = ROWS + 16
-CHUNKS = 8
+CHUNKS = 4
 EARLY = 32
 BLOCK = 32
 CUBE_ROOT_2 = 2.0 ** (1.0 / 3.0)
@@ -141,6 +141,7 @@
     index_smem,
     outgoing,
     incoming,
+    rim_columns,
     rim_out,
     rim_in,
     rows_out,
@@ -170,7 +171,7 @@
     per_chunk = ROWS // CHUNKS
 
     def plane(k, layer):
-        return (k * (LAYERS + 2) + layer) * PLANE
+        return (k * (LAYERS + 2) + layer) * ROWS
 
     small = [
         pltpu.make_async_copy(owner_hbm, owner, small_sem.at[0]),
@@ -180,7 +181,7 @@
         copy.start()
     faces = [
         pltpu.make_async_copy(
-            moments_hbm.at[k, interface], face.at[pl.ds(k * ROWS, ROWS)], cell_sem.at[k]
+            moments_hbm.at[k, pl.ds(pl.multiple_of(interface * ROWS, ROWS), ROWS)], face.at[pl.ds(k * ROWS, ROWS)], cell_sem.at[k]
         )
         for k in range(MOMENTS)
     ]
@@ -196,14 +197,13 @@
     ]
     body_copies = []
     for k in range(MOMENTS):
-        for layer in range(LAYERS):
-            body_copies.append(
-                pltpu.make_async_copy(
-                    moments_hbm.at[k, layer],
-                    cells.at[pl.ds(plane(k, layer + 1) + 8, ROWS)],
-                    cell_sem.at[MOMENTS + k * LAYERS + layer],
-                )
+        body_copies.append(
+            pltpu.make_async_copy(
+                moments_hbm.at[k],
+                cells.at[pl.ds(plane(k, 1), LAYERS * ROWS)],
+                cell_sem.at[MOMENTS + k],
             )
+        )
     fields = [
         pltpu.make_async_copy(source, destination, small_sem.at[2 + i])
         for i, (source, destination) in enumerate(
@@ -241,7 +241,7 @@
         index = ROWS + jnp.sum(jnp.where(chosen, sublane - ROWS, 0), axis=0, keepdims=True)
         index_vmem[r : r + 1, :] = index
         row = jnp.sum(jnp.where(chosen, target_column, 0), axis=0, keepdims=True)
-        rows_out[pl.ds(r * DEPTH + depth, 1), :] = row
+        rows_out[r, pl.ds(depth, 1), :] = row
     to_scalar = pltpu.make_async_copy(index_vmem, index_smem, small_sem.at[6])
     to_scalar.start()
 
@@ -276,16 +276,15 @@
     pl.semaphore_wait(barrier, PEERS + len(near))
 
     for peer in column:
-        for r in range(SLOTS):
-            row = rows_out.at[pl.ds(r * DEPTH + depth, 1)]
-            pltpu.make_async_remote_copy(
-                src_ref=row,
-                dst_ref=row,
-                send_sem=hop_send_sem,
-                recv_sem=hop_recv_sem,
-                device_id=(region, peer),
-                device_id_type=MESH,
-            ).start()
+        row = rows_out.at[:, pl.ds(depth, 1)]
+        pltpu.make_async_remote_copy(
+            src_ref=row,
+            dst_ref=row,
+            send_sem=hop_send_sem,
+            recv_sem=hop_recv_sem,
+            device_id=(region, peer),
+            device_id_type=MESH,
+        ).start()
 
     def dispatch(peer, carry):
         for r in range(SLOTS):
@@ -312,12 +311,13 @@
         for k in range(MOMENTS):
             for layer in range(LAYERS):
                 p = k * LAYERS + layer
-                values = cells[pl.ds(pl.multiple_of(plane(k, layer + 1) + 8 + i * 8, 8), 8), :]
+                values = cells[pl.ds(pl.multiple_of(plane(k, layer + 1) + i * 8, 8), 8), :]
                 packed = jnp.where(lanes == p, pltpu.roll(values, p + 1, 1), packed)
-        rim_out[pl.ds(pl.multiple_of(i * 8, 8), 8), :] = packed
+        rim_columns[pl.ds(pl.multiple_of(i * 8, 8), 8), :] = packed
         return carry
 
     lax.fori_loop(0, ROWS // 8, pack, 0, unroll=4)
+    rim_out[...] = rim_columns[...].T[:PLANES]
     rim = pltpu.make_async_remote_copy(
         src_ref=rim_out,
         dst_ref=rim_in,
@@ -331,8 +331,8 @@
     lax.fori_loop(0, PEERS, dispatch, 0, unroll=2)
 
     hop = pltpu.make_async_remote_copy(
-        src_ref=rows_out.at[pl.ds(0, SLOTS * (DEPTH - 1))],
-        dst_ref=rows_out.at[pl.ds(0, SLOTS * (DEPTH - 1))],
+        src_ref=rows_out.at[:, pl.ds(0, DEPTH - 1)],
+        dst_ref=rows_out.at[:, pl.ds(0, DEPTH - 1)],
         send_sem=hop_send_sem,
         recv_sem=hop_recv_sem,
         device_id=(region, after),
@@ -341,36 +341,29 @@
     hop.wait_recv()
 
     def spread(i, carry):
-        for r in range(SLOTS):
-            pltpu.make_async_remote_copy(
-                src_ref=rows_out.at[pl.ds(r * DEPTH, DEPTH)],
-                dst_ref=rows_in.at[pl.ds(r * PEERS + flat * DEPTH, DEPTH)],
-                send_sem=rows_send_sem,
-                recv_sem=rows_recv_sem,
-                device_id=(other, depth * FLAT + i),
-                device_id_type=MESH,
-            ).start()
+        pltpu.make_async_remote_copy(
+            src_ref=rows_out,
+            dst_ref=rows_in.at[:, pl.ds(pl.multiple_of(flat * DEPTH, DEPTH), DEPTH)],
+            send_sem=rows_send_sem,
+            recv_sem=rows_recv_sem,
+            device_id=(other, depth * FLAT + i),
+            device_id_type=MESH,
+        ).start()
         return carry
 
     lax.fori_loop(0, FLAT, spread, 0)
 
-    zero_rows = jnp.zeros((8, FACES), F32)
-
-    def edges(i, carry):
-        base = pl.multiple_of(i * PLANE, 8)
-        cells[pl.ds(base, 8), :] = zero_rows
-        cells[pl.ds(base + 8 + ROWS, 8), :] = zero_rows
-        return carry
-
-    lax.fori_loop(0, MOMENTS * (LAYERS + 2), edges, 0)
     for k in range(MOMENTS):
-        empty = plane(k, (LAYERS + 1) * region)
-        cells[pl.ds(empty + 8, ROWS), :] = jnp.zeros((ROWS, FACES), F32)
+        for edge in (0, LAYERS + 1):
+            cells[pl.ds(plane(k, edge), ROWS), :] = jnp.zeros((ROWS, FACES), F32)
 
     for copy in fields:
         copy.wait()
     rim.wait_recv()
+    unused = jnp.zeros((FACES - PLANES, ROWS), F32)
+    rim_columns[...] = jnp.concatenate([rim_in[...], unused], axis=0).T
     lanes_block = lax.broadcasted_iota(jnp.int32, (BLOCK, FACES), 1)
+    rows_block = lax.broadcasted_iota(jnp.int32, (BLOCK, FACES), 0)
 
     def advect(layer, i, at_interface):
         start = pl.multiple_of(i * BLOCK, BLOCK)
@@ -383,14 +376,16 @@
         cr = jnp.abs(cr)
         cz = jnp.abs(cz)
         keep = 1.0 - ca - cr - cz
-        rims = rim_in[pl.ds(start, BLOCK), :]
+        at_edge = rows_block + start == jnp.where(upward, 0, ROWS - 1)
+        cz = jnp.where(at_edge, 0.0, cz)
+        rims = rim_columns[pl.ds(start, BLOCK), :]
         if at_interface:
             from_ghost = outward == (region == 1)
             ghost_weight[pl.ds(start, BLOCK), :] = jnp.where(from_ghost, cr, 0.0)
             cr = jnp.where(from_ghost, 0.0, cr)
         advected = []
         for k in range(MOMENTS):
-            row = plane(k, layer + 1) + 8 + start
+            row = plane(k, layer + 1) + start
             m = cells[pl.ds(row, BLOCK), :]
             shift = lax.rem(2 * FACES - (k * LAYERS + layer), FACES)
             previous = jnp.where(
@@ -399,10 +394,10 @@
             axial_below = cells[pl.ds(row - 1, BLOCK), :]
             axial_beyond = cells[pl.ds(row + 1, BLOCK), :]
             if at_interface:
-                radial_side = cells[pl.ds(row + (2 * region - 1) * PLANE, BLOCK), :]
+                radial_side = cells[pl.ds(row + (2 * region - 1) * ROWS, BLOCK), :]
             else:
-                below = cells[pl.ds(row - PLANE, BLOCK), :]
-                beyond = cells[pl.ds(row + PLANE, BLOCK), :]
+                below = cells[pl.ds(row - ROWS, BLOCK), :]
+                beyond = cells[pl.ds(row + ROWS, BLOCK), :]
                 radial_side = jnp.where(outward, below, beyond)
             advected.append(
                 keep * m
@@ -446,7 +441,7 @@
     rows.wait_recv()
     mine = []
     for r in range(SLOTS):
-        named = jnp.where(lane == me, rows_in[pl.ds(r * PEERS, PEERS), :], 0)
+        named = jnp.where(lane == me, rows_in[r], 0)
         named = jnp.sum(named, axis=1, keepdims=True)
         mine.append(jnp.where(named == lane, 1.0, 0.0).T)
     hits = jnp.concatenate(mine, axis=1).astype(BF16)
@@ -505,7 +500,7 @@
         in_specs=[pl.BlockSpec(memory_space=pltpu.HBM)] * 8,
         out_specs=pl.BlockSpec(memory_space=pltpu.VMEM),
         scratch_shapes=[
-            pltpu.VMEM((MOMENTS * (LAYERS + 2) * PLANE, FACES), F32),
+            pltpu.VMEM((MOMENTS * (LAYERS + 2) * ROWS, FACES), F32),
             pltpu.VMEM(field, F32),
             pltpu.VMEM(field, F32),
             pltpu.VMEM(field, F32),
@@ -520,13 +515,14 @@
             pltpu.VMEM((MESSAGE * PEERS, FACES), F32),
             pltpu.VMEM((MESSAGE * PEERS, FACES), F32),
             pltpu.VMEM((ROWS, FACES), F32),
-            pltpu.VMEM((ROWS, FACES), F32),
-            pltpu.VMEM((SLOTS * DEPTH, PEERS), jnp.int32),
-            pltpu.VMEM((SLOTS * PEERS, PEERS), jnp.int32),
+            pltpu.VMEM((PLANES, ROWS), F32),
+            pltpu.VMEM((PLANES, ROWS), F32),
+            pltpu.VMEM((SLOTS, DEPTH, PEERS), jnp.int32),
+            pltpu.VMEM((SLOTS, PEERS, PEERS), jnp.int32),
             pltpu.VMEM((MOMENTS * ROWS, FACES), F32),
             pltpu.VMEM((ROWS, FACES), F32),
             dma((7,)),
-            dma((MOMENTS + MOMENTS * LAYERS,)),
+            dma((2 * MOMENTS,)),
             dma((CHUNKS,)),
             dma,
             dma,
@@ -545,7 +541,7 @@
         *[
             pltpu.with_memory_space_constraint(operand, pltpu.HBM)
             for operand in (
-                moments.reshape(shape),
+                moments.reshape(MOMENTS, LAYERS * ROWS, FACES),
                 courant_azimuth.reshape(field),
                 courant_radial.reshape(field),
                 courant_axial.reshape(field),

time: 36.7 us -> 34.7 us (0.946)
  Pallas kernels: 35.5 us -> 33.4 us
    pallas_call x1, Pallas kernels: 35.5 us -> 33.4 us  [on_device(): pl.pallas_call(kernel, out_shape=jax.ShapeDtypeStruct(shape, F32), in_spe...]
where the time goes in v5:
time: 34.7 us; the launch traced here: 34.6 us
  Pallas kernels  33.4 us (96%)
  local copies, waits for them, and re-layouts  1.15 us (3%)
    pallas_call x1, Pallas kernels, on_device(): pl.pallas_call(kernel, out_shape=jax.ShapeDtypeStruct(shape, F32), in_spe...  33.4 us
    unnamed x1, local copies, waits for them, and re-layouts  1.15 us

profile of v5, /device:TPU:65, one launch (start us, length us, event | category | flops | bytes accessed | tf_op | source)
XLA Modules:
  0.0 34.6 jit_solution(14329670299325002699)
XLA Ops:
  0.0 33.4 %transport.1 = f32[6,4,128,128]{3,2,1,0:T(8,128)S(1)} custom-call(f32[6,512,128]{2,1,0:T(8,128)} %bitcast.10, f32[512,128]{1,0:T(8,128)} %bitcast.11, f32[512,128]{1,0:T(8,128)} %bitcast.12, f32[512,128]{1,0:T(8,128)} %bitcast.13, f32[512,128]{1,0:T(8,128)} %bitcast.14, s32[1,128]{1,0:T(1,128)} %bitcast.15, s32[1,128]{1,0:T(1,128)} %target_hbm.1, ...), custom_call_target="tpu_custom_call" | custom-call | tf_op jit(solution)/shard_map/transport/pallas_call | solution.py:497
  33.4 1.1 %copy.10 = f32[1,6,4,128,128]{4,3,2,1,0:T(8,128)} copy(f32[1,6,4,128,128]{4,3,2,1,0:T(8,128)S(1)} %bitcast.8) | data formatting | bytes 3145728

commit v6 on v5

--- a/solution.py
+++ b/solution.py
@@ -210,7 +210,7 @@
             ((azimuth_hbm, azimuth), (radial_hbm, radial), (axial_hbm, axial), (shear_hbm, shear))
         )
     ]
-    for copy in chunks + body_copies + fields:
+    for copy in chunks[:-1] + body_copies + chunks[-1:] + fields:
         copy.start()
 
     barrier = pltpu.get_barrier_semaphore()
@@ -268,7 +268,27 @@
         )
         return carry
 
-    for c in range(CHUNKS):
+    for c in range(CHUNKS - 1):
+        chunks[c].wait()
+        lax.fori_loop(c * per_chunk, (c + 1) * per_chunk, weigh, 0, unroll=per_chunk)
+
+    for copy in body_copies:
+        copy.wait()
+    lanes = lax.broadcasted_iota(jnp.int32, (8, FACES), 1)
+
+    def pack(i, carry):
+        packed = jnp.zeros((8, FACES), F32)
+        for k in range(MOMENTS):
+            for layer in range(LAYERS):
+                p = k * LAYERS + layer
+                values = cells[pl.ds(pl.multiple_of(plane(k, layer + 1) + i * 8, 8), 8), :]
+                packed = jnp.where(lanes == p, pltpu.roll(values, p + 1, 1), packed)
+        rim_columns[pl.ds(pl.multiple_of(i * 8, 8), 8), :] = packed
+        return carry
+
+    lax.fori_loop(0, ROWS // 8, pack, 0, unroll=4)
+    rim_out[...] = rim_columns[...].T[:PLANES]
+    for c in range(CHUNKS - 1, CHUNKS):
         chunks[c].wait()
         lax.fori_loop(c * per_chunk, (c + 1) * per_chunk, weigh, 0, unroll=per_chunk)
     to_scalar.wait()
@@ -302,22 +322,6 @@
         return carry
 
 
-    for copy in body_copies:
-        copy.wait()
-    lanes = lax.broadcasted_iota(jnp.int32, (8, FACES), 1)
-
-    def pack(i, carry):
-        packed = jnp.zeros((8, FACES), F32)
-        for k in range(MOMENTS):
-            for layer in range(LAYERS):
-                p = k * LAYERS + layer
-                values = cells[pl.ds(pl.multiple_of(plane(k, layer + 1) + i * 8, 8), 8), :]
-                packed = jnp.where(lanes == p, pltpu.roll(values, p + 1, 1), packed)
-        rim_columns[pl.ds(pl.multiple_of(i * 8, 8), 8), :] = packed
-        return carry
-
-    lax.fori_loop(0, ROWS // 8, pack, 0, unroll=4)
-    rim_out[...] = rim_columns[...].T[:PLANES]
     rim = pltpu.make_async_remote_copy(
         src_ref=rim_out,
         dst_ref=rim_in,

time: 34.7 us -> 34.7 us (level)
  no operation moved by 1% of the time
where the time goes in v6:
time: 34.7 us; the launch traced here: 34.6 us
  Pallas kernels  33.5 us (97%)
  local copies, waits for them, and re-layouts  1.15 us (3%)
    pallas_call x1, Pallas kernels, on_device(): pl.pallas_call(kernel, out_shape=jax.ShapeDtypeStruct(shape, F32), in_spe...  33.5 us
    unnamed x1, local copies, waits for them, and re-layouts  1.15 us

profile of v6, /device:TPU:65, one launch (start us, length us, event | category | flops | bytes accessed | tf_op | source)
XLA Modules:
  0.0 34.6 jit_solution(13438932857216818186)
XLA Ops:
  0.0 33.5 %transport.1 = f32[6,4,128,128]{3,2,1,0:T(8,128)S(1)} custom-call(f32[6,512,128]{2,1,0:T(8,128)} %bitcast.10, f32[512,128]{1,0:T(8,128)} %bitcast.11, f32[512,128]{1,0:T(8,128)} %bitcast.12, f32[512,128]{1,0:T(8,128)} %bitcast.13, f32[512,128]{1,0:T(8,128)} %bitcast.14, s32[1,128]{1,0:T(1,128)} %bitcast.15, s32[1,128]{1,0:T(1,128)} %target_hbm.1, ...), custom_call_target="tpu_custom_call" | custom-call | tf_op jit(solution)/shard_map/transport/pallas_call | solution.py:501
  33.5 1.1 %copy.10 = f32[1,6,4,128,128]{4,3,2,1,0:T(8,128)} copy(f32[1,6,4,128,128]{4,3,2,1,0:T(8,128)S(1)} %bitcast.8) | data formatting | bytes 3145728
